TPU v7x, 32 devices: a whole 2x2x4 slice. The times are simulated.
32 devices in a mesh: atoms: 4 (over y, x), energy: 8 (over z, core).
Axes of the slice: x: 2, y: 2, z: 4, core: 2. Of those that a mesh axis runs over, the one named last changes fastest.
Arguments:
- retarded_green_blocks: bfloat16 [4, 24, 2, 384, 384], P('atoms', 'energy'), may hold values from -0.21875 to 0.21875
- contact_lesser_sigma: bfloat16 [4, 24, 2, 384, 384], P('atoms', 'energy'), may hold values from -6 to 6
- energy_counts: int32 [8], replicated, may hold values from 1 to 3, 15 in all
- phonon_shift: int32 [64], replicated, may hold values from 1 to 7
- phonon_weight: float32 [4, 64], replicated, may hold values from 0.01 to 0.1
Outputs:
- scattered: bfloat16 [4, 24, 2, 384, 384], P('atoms', 'energy')
Inputs may be any that keep to these rules, and one draw needn't show every extreme that they name: energy_counts sums to 15; its largest entry is exactly 3.
All inputs are finite; a program needn't handle non-finite values.
Results may differ from a plain program's by a relative error of at most 0.007.
Values may be sent and summed in bfloat16 or wider, within the bound.
A program may use at most 64 MiB of HBM per device.

v0:
```python
import jax
import jax.numpy as jnp
from jax import lax
from jax.sharding import PartitionSpec as P


def extended(value, sides, width):
    for axis, dim in sides:
        size, length = (lax.axis_size(axis), value.shape[dim])
        up = [(i, (i + 1) % size) for i in range(size - 1)]
        down = [(j, i) for i, j in up]
        last = lax.slice_in_dim(value, length - width, length, axis=dim)
        leading = lax.slice_in_dim(value, 0, width, axis=dim)
        before = lax.ppermute(last, axis, up)
        after = lax.ppermute(leading, axis, down)
        value = jnp.concatenate([before, value, after], axis=dim)
    return value


def complex_product(left, right):
    prods = jnp.einsum("spik,sqkj->spqij", left, right, preferred_element_type=jnp.float32)
    return jnp.stack([prods[:, 0, 0] - prods[:, 1, 1], prods[:, 0, 1] + prods[:, 1, 0]], axis=1)


def product_adjoint(left, right):
    prods = jnp.einsum("spik,sqjk->spqij", left, right, preferred_element_type=jnp.float32)
    return jnp.stack([prods[:, 0, 0] + prods[:, 1, 1], prods[:, 1, 0] - prods[:, 0, 1]], axis=1)


def kernels(energy_counts, phonon_shift, phonon_weight, groups, per_group):
    total_slots = groups * per_group
    starts = jnp.cumsum(energy_counts) - energy_counts
    start_slot = jnp.broadcast_to(starts[:, None], (groups, per_group)).reshape(total_slots)
    slot_tally = jnp.broadcast_to(energy_counts[:, None], (groups, per_group)).reshape(total_slots)
    within = jnp.arange(total_slots, dtype=jnp.int32) % per_group
    energy_index = start_slot + within
    live = (within < slot_tally).astype(jnp.float32)
    spacing = energy_index[None, :] - energy_index[:, None]
    upward = (spacing[:, :, None] == phonon_shift[None, None, :]).astype(jnp.float32)
    downward = (spacing[:, :, None] == -phonon_shift[None, None, :]).astype(jnp.float32)
    mask = live[:, None] * live[None, :]
    own_kernel = jnp.sum(upward * phonon_weight[0] + downward * phonon_weight[1], axis=-1) * mask
    side_kernel = jnp.sum(upward * phonon_weight[2] + downward * phonon_weight[3], axis=-1) * mask
    return (own_kernel.astype(jnp.bfloat16), side_kernel.astype(jnp.bfloat16))


def on_device(
    retarded_green_blocks, contact_lesser_sigma, energy_counts, phonon_shift, phonon_weight
):
    groups = lax.axis_size("energy")
    per_group = retarded_green_blocks.shape[1]
    retarded = retarded_green_blocks[0]
    mixed = complex_product(retarded, contact_lesser_sigma[0]).astype(jnp.bfloat16)
    lesser = product_adjoint(mixed, retarded).astype(jnp.bfloat16)[None]
    own_kernel, side_kernel = kernels(energy_counts, phonon_shift, phonon_weight, groups, per_group)
    moved = lax.all_to_all(lesser, "energy", split_axis=3, concat_axis=1, tiled=True)
    regrouped = extended(moved, (("atoms", 0),), 1)
    slot_count = regrouped.shape[1]
    columns = regrouped.shape[2] * regrouped.shape[3] * regrouped.shape[4]
    flat = regrouped.reshape(3, slot_count, columns)
    sigma = jnp.dot(own_kernel, flat[1], preferred_element_type=jnp.float32)
    sigma = sigma + jnp.dot(side_kernel, flat[0], preferred_element_type=jnp.float32)
    sigma = sigma + jnp.dot(side_kernel, flat[2], preferred_element_type=jnp.float32)
    sigma = sigma.astype(jnp.bfloat16).reshape((1,) + regrouped.shape[1:])
    returned = lax.all_to_all(sigma, "energy", split_axis=1, concat_axis=3, tiled=True)
    result = complex_product(retarded, returned[0]).astype(jnp.bfloat16)
    return result[None]


def solution(mesh):
    in_specs = (
        P("atoms", "energy", None, None, None),
        P("atoms", "energy", None, None, None),
        P(),
        P(),
        P(),
    )
    out_specs = P("atoms", "energy", None, None, None)
    return jax.shard_map(
        on_device, mesh=mesh, in_specs=in_specs, out_specs=out_specs, check_vma=False
    )
```

profile of v0, /device:TPU:0, one launch (start us, length us, event | category | flops | bytes accessed | tf_op | source)
XLA Modules:
  0.0 195.5 jit_solution(2721880612030138604)
XLA Ops:
  0.0 1.5 copy-done
  1.5 3.6 %convolution_bitcast_fusion.2 = f32[3,2,2,384,384]{3,4,1,2,0:T(8,128)S(1)} fusion(bf16[1,3,2,384,384]{4,3,2,1,0:T(8,128)(2,1)} %param.6, bf16[1,3,2,384,384]{4,3,2,1,0:T(8,128)(2,1)S(1)} %copy-done), kind=kOutput, calls=%fused_computation.5 | convolution fusion | flops 1358954496 | bytes 10616832 | tf_op jit(solution)/shard_map/spik,sqkj->spqij/dot_general | solution.py:21
  5.3 0.2 fusion.15
  5.5 2.2 %convolution_bitcast_fusion.1 = f32[3,2,2,384,384]{4,3,2,1,0:T(8,128)S(1)} fusion(bf16[1,3,2,384,384]{4,3,2,1,0:T(8,128)(2,1)S(1)} %copy-done, bf16[3,1,384,384]{2,3,0,1:T(8,128)(2,1)S(1)} %fusion.16, bf16[3,1,384,384]{2,3,0,1:T(8,128)(2,1)S(1)} %fusion.15), kind=kOutput, calls=%fused_computation.4 | convolution fusion | flops 1359839232 | bytes 10616832 | tf_op jit(solution)/shard_map/spik,sqjk->spqij/dot_general | solution.py:26
  7.7 0.2 fusion.18
  8.1 0.2 pad_maximum_fusion
  8.3 1.8 copy.90
  10.1 48.2 %all_to_all.33 = bf16[1,3,2,384,384]{4,2,1,0,3:T(2,128)(2,1)S(1)} all-to-all(bf16[1,3,2,384,384]{4,2,1,0,3:T(2,128)(2,1)S(1)} %copy.90), channel_id=1, replica_groups=mesh['atoms'=4,'energy'=8] {'energy'}, dimensions={3} | all-to-all | bytes 3538944 | tf_op jit(solution)/shard_map/all_to_all | solution.py:56
  58.3 0.2 copy.91
  58.8 4.6 %collective-permute-start = (bf16[1,24,2,48,384]{4,3,2,1,0:T(8,128)(2,1)S(1)}, bf16[1,24,2,48,384]{4,3,2,1,0:T(8,128)(2,1)}, u32[]{:S(2)}, u32[]{:S(2)}) collective-permute-start(bf16[1,24,2,48,384]{4,3,2,1,0:T(8,128)(2,1)S(1)} %bitcast.119), channel_id=1, source_target_pairs={{0,8},{8,16},{16,24},{1,9},{9,17},{17,25},{2,10},{10,18},{18,26},{... | collective-permute-start | bytes 5308424 | tf_op jit(solution)/shard_map/ppermute | solution.py:14
  63.4 0.5 neg.4
  64.2 0.6 reshape.326
  64.8 0.7 reshape.327
  65.5 1.3 collective-permute-start.1
  66.8 0.6 fusion.31
  67.5 1.6 fusion.24
  69.1 0.7 compare_convert_fusion
  69.8 2.2 %squeeze.14 = bf16[24,36864]{1,0:T(8,128)(2,1)} reshape(bf16[1,8,3,2,48,384]{5,4,3,2,1,0:T(8,128)(2,1)S(1)} %copy.92) | data formatting | bytes 3538944 | tf_op jit(solution)/shard_map/squeeze | solution.py:61
  72.0 4.0 %fusion.27 = f32[24,36864]{1,0:T(8,128)} fusion(bf16[24,36864]{1,0:T(8,128)(2,1)} %squeeze.14, f32[24,24]{1,0:T(8,128)} %get-tuple-element.6, f32[24]{0:T(128)S(1)} %compare_convert_fusion), kind=kOutput, calls=%fused_computation.50 | convolution fusion | flops 42469056 | bytes 5310816 | tf_op jit(solution)/shard_map/dot_general | solution.py:61
  76.0 23.7 %collective-permute-done = bf16[1,24,2,48,384]{4,3,2,1,0:T(8,128)(2,1)} collective-permute-done((bf16[1,24,2,48,384]{4,3,2,1,0:T(8,128)(2,1)S(1)}, bf16[1,24,2,48,384]{4,3,2,1,0:T(8,128)(2,1)}, u32[]{:S(2)}, u32[]{:S(2)}) %collective-permute-start) | collective-permute-done | bytes 1769504 | tf_op jit(solution)/shard_map/ppermute | solution.py:14
  99.7 3.9 %squeeze.15 = bf16[24,36864]{1,0:T(8,128)(2,1)} reshape(bf16[1,24,2,48,384]{4,3,2,1,0:T(8,128)(2,1)} %collective-permute-done) | data formatting | bytes 3538944 | tf_op jit(solution)/shard_map/squeeze | solution.py:62
  103.7 5.0 %convolution_add_fusion.1 = f32[24,36864]{1,0:T(8,128)} fusion(f32[24,36864]{1,0:T(8,128)} %fusion.27, bf16[24,36864]{1,0:T(8,128)(2,1)} %squeeze.15, f32[24,24]{1,0:T(8,128)S(1)} %get-tuple-element.5, f32[24]{0:T(128)S(1)} %compare_convert_fusion), kind=kOutput, calls=%fused_computation.1 | convolution fusion | flops 43353792 | bytes 8849760 | tf_op jit(solution)/shard_map/dot_general | solution.py:62
  108.7 31.0 %collective-permute-done.1 = bf16[1,24,2,48,384]{4,3,2,1,0:T(8,128)(2,1)} collective-permute-done((bf16[1,24,2,48,384]{4,3,2,1,0:T(8,128)(2,1)S(1)}, bf16[1,24,2,48,384]{4,3,2,1,0:T(8,128)(2,1)}, u32[]{:S(2)}, u32[]{:S(2)}) %collective-permute-start.1) | collective-permute-done | bytes 1769504 | tf_op jit(solution)/shard_map/ppermute | solution.py:15
  139.7 2.7 %squeeze.16 = bf16[24,36864]{1,0:T(8,128)(2,1)S(1)} reshape(bf16[1,24,2,48,384]{4,3,2,1,0:T(8,128)(2,1)} %collective-permute-done.1) | data formatting | bytes 3538944 | tf_op jit(solution)/shard_map/squeeze | solution.py:63
  142.4 2.7 %fusion = bf16[24,36864]{1,0:T(8,128)(2,1)S(1)} fusion(f32[24,36864]{1,0:T(8,128)} %convolution_add_fusion.1, bf16[24,36864]{1,0:T(8,128)(2,1)S(1)} %squeeze.16, f32[24,24]{1,0:T(8,128)S(1)} %get-tuple-element.5, f32[24]{0:T(128)S(1)} %compare_convert_fusion), kind=kOutput, calls=%fused_computation.2 | convolution fusion | flops 44238528 | bytes 7080288 | tf_op jit(solution)/shard_map/dot_general | solution.py:63
  145.1 0.2 copy.116
  145.3 44.9 %all_to_all.34 = bf16[1,24,2,48,384]{4,3,2,0,1:T(8,128)(2,1)S(1)} all-to-all(bf16[1,24,2,48,384]{4,3,2,0,1:T(8,128)(2,1)S(1)} %bitcast.122), channel_id=1, replica_groups=mesh['atoms'=4,'energy'=8] {'energy'}, dimensions={1} | all-to-all | bytes 3538944 | tf_op jit(solution)/shard_map/all_to_all | solution.py:65
  190.2 0.2 copy.95
  190.4 2.2 %convolution_bitcast_fusion = f32[3,2,2,384,384]{3,4,1,2,0:T(8,128)S(1)} fusion(bf16[3,2,384,384,1]{3,2,4,1,0:T(8,128)(2,1)S(1)} %bitcast.125, bf16[1,3,2,384,384]{4,3,2,1,0:T(8,128)(2,1)S(1)} %copy-done), kind=kOutput, calls=%fused_computation.3 | convolution fusion | flops 1358954496 | bytes 10616832 | tf_op jit(solution)/shard_map/spik,sqkj->spqij/dot_general | solution.py:21
  192.8 0.2 fusion.19
  193.0 0.2 pad_maximum_fusion.1
  193.2 2.3 %copy.99 = bf16[1,3,2,384,384]{4,3,2,1,0:T(8,128)(2,1)} copy(bf16[1,3,2,384,384]{3,4,1,2,0:T(8,128)(2,1)S(1)} %pad_maximum_fusion.1) | data formatting | bytes 3538944 | tf_op jit(solution)/shard_map/stack | solution.py:22
  (17 shorter events, 1.1 us)
Async XLA Ops:
  0.0 1.5 copy-start
  58.5 4.9 %copy-start.2 = (s32[64]{0:T(128)S(1)}, s32[64]{0:T(128)}, u32[]{:S(2)}) copy-start(s32[64]{0:T(128)} %param.8) | copy-start | bytes 772
  58.6 5.4 %copy-start.3 = (s32[8]{0:T(128)S(1)}, s32[8]{0:T(128)}, u32[]{:S(2)}) copy-start(s32[8]{0:T(128)} %param.7) | copy-start | bytes 100
  58.6 8.8 %copy-start.1 = (f32[4,64]{1,0:T(4,128)S(1)}, f32[4,64]{1,0:T(4,128)}, u32[]{:S(2)}) copy-start(f32[4,64]{1,0:T(4,128)} %param.9) | copy-start | bytes 3076
  58.8 41.0 %collective-permute-start = (bf16[1,24,2,48,384]{4,3,2,1,0:T(8,128)(2,1)S(1)}, bf16[1,24,2,48,384]{4,3,2,1,0:T(8,128)(2,1)}, u32[]{:S(2)}, u32[]{:S(2)}) collective-permute-start(bf16[1,24,2,48,384]{4,3,2,1,0:T(8,128)(2,1)S(1)} %bitcast.119), channel_id=1, source_target_pairs={{0,8},{8,16},{16,24},{1,9},{9,17},{17,25},{2,10},{10,18},{18,26},{... | collective-permute-start | bytes 5308424 | tf_op jit(solution)/shard_map/ppermute | solution.py:14
  65.5 74.2 %collective-permute-start.1 = (bf16[1,24,2,48,384]{4,3,2,1,0:T(8,128)(2,1)S(1)}, bf16[1,24,2,48,384]{4,3,2,1,0:T(8,128)(2,1)}, u32[]{:S(2)}, u32[]{:S(2)}) collective-permute-start(bf16[1,24,2,48,384]{4,3,2,1,0:T(8,128)(2,1)S(1)} %bitcast.120), channel_id=1, source_target_pairs={{8,0},{16,8},{24,16},{9,1},{17,9},{25,17},{10,2},{18,10},{26,18},{... | collective-permute-start | bytes 5308424 | tf_op jit(solution)/shard_map/ppermute | solution.py:15
where the time goes:
time: 196 us; the launch traced here: 195 us
  blocking collectives  93 us (47%)
  waiting for transfers between devices  54.8 us (28%)
  matrix products  19.8 us (10%)
  local copies, waits for them, and re-layouts  16.6 us (8%)
  starting transfers between devices  5.92 us (3%)
  other arithmetic  5.25 us (3%)
    all_to_all x1, blocking collectives, on_device(): lax.all_to_all(lesser, 'energy', split_axis=3, concat_axis=1, tiled=True)  48.2 us
    all_to_all x1, blocking collectives, on_device(): lax.all_to_all(sigma, 'energy', split_axis=1, concat_axis=3, tiled=True)  44.9 us
    ppermute x1, waiting for transfers between devices, extended(): after = lax.ppermute(leading, axis, down)  31 us
    ppermute x1, waiting for transfers between devices, extended(): before = lax.ppermute(last, axis, up)  23.7 us
    dot_general x2, matrix products, complex_product(): jnp.einsum('spik,sqkj->spqij', left, right, preferred_element_type=jnp.fl...  5.83 us
    dot_general x1, matrix products, on_device(): jnp.dot(side_kernel, flat[0], preferred_element_type=jnp.float32)  5.02 us
    ppermute x1, starting transfers between devices, extended(): before = lax.ppermute(last, axis, up)  4.64 us
    dot_general x1, matrix products, on_device(): sigma = jnp.dot(own_kernel, flat[1], preferred_element_type=jnp.float32)  4.04 us
  transfers between devices with their start and end apart: 2, of which 2 were waited for; matrix products, arithmetic and copies ran while one was open for 10% of the time, Pallas kernels for 0%

commit v1 on v0

--- a/solution.py
+++ b/solution.py
@@ -2,6 +2,7 @@
 import jax.numpy as jnp
 from jax import lax
 from jax.sharding import PartitionSpec as P
+from jax.lax import axis_index, axis_size, ppermute
 
 
 def extended(value, sides, width):
@@ -62,7 +63,16 @@
     sigma = sigma + jnp.dot(side_kernel, flat[0], preferred_element_type=jnp.float32)
     sigma = sigma + jnp.dot(side_kernel, flat[2], preferred_element_type=jnp.float32)
     sigma = sigma.astype(jnp.bfloat16).reshape((1,) + regrouped.shape[1:])
-    returned = lax.all_to_all(sigma, "energy", split_axis=1, concat_axis=3, tiled=True)
+    formed, y2 = (axis_size("energy"), axis_index("energy"))
+    state_now = sigma.shape[1] // formed
+    left_arr = jnp.roll(sigma, shift=-y2 * state_now, axis=1)
+    found = [lax.slice_in_dim(left_arr, 0, state_now, axis=1)]
+    for dev_i in [*range(1, formed)]:
+        d_next = lax.slice_in_dim(left_arr, dev_i * state_now, (dev_i + 1) * state_now, axis=1)
+        found.append(
+            ppermute(d_next, "energy", [(to_i, (to_i + dev_i) % formed) for to_i in range(formed)])
+        )
+    returned = jnp.roll(jnp.concatenate(found[::-1], axis=3), (y2 + 1) * found[0].shape[3], axis=3)
     result = complex_product(retarded, returned[0]).astype(jnp.bfloat16)
     return result[None]
 

time: 196 us -> 194 us (0.990)
  blocking collectives: 93 us -> 48.2 us
  waiting for transfers between devices: 54.8 us -> 85.8 us
  local copies, waits for them, and re-layouts: 16.6 us -> 21.9 us
  starting transfers between devices: 5.92 us -> 11.2 us
    all_to_all x1 -> x0, blocking collectives: 44.9 us -> none  [on_device(): lax.all_to_all(sigma, 'energy', split_axis=1, concat_axis=3, tiled=True)]
    ppermute x0 -> x7, waiting for transfers between devices: none -> 31.2 us  [on_device(): ppermute(d_next, 'energy', [(to_i, (to_i + dev_i) % formed) for to_i in r...]
    ppermute x0 -> x7, starting transfers between devices: none -> 5.15 us  [on_device(): ppermute(d_next, 'energy', [(to_i, (to_i + dev_i) % formed) for to_i in r...]
    unnamed x9 -> x24, local copies, waits for them, and re-layouts: 1.74 us -> 6.03 us
  transfers between devices with their start and end apart: 2 -> 9, of which waited for: 2 -> 6; matrix products, arithmetic and copies ran while one was open for 10% -> 12% of each run, Pallas kernels for 0% -> 0%
where the time goes in v1:
time: 194 us; the launch traced here: 193 us
  waiting for transfers between devices  85.8 us (44%)
  blocking collectives  48.2 us (25%)
  local copies, waits for them, and re-layouts  21.9 us (11%)
  matrix products  19.8 us (10%)
  starting transfers between devices  11.2 us (6%)
  other arithmetic  5.99 us (3%)
    all_to_all x1, blocking collectives, on_device(): lax.all_to_all(lesser, 'energy', split_axis=3, concat_axis=1, tiled=True)  48.2 us
    ppermute x7, waiting for transfers between devices, on_device(): ppermute(d_next, 'energy', [(to_i, (to_i + dev_i) % formed) for to_i in r...  31.2 us
    ppermute x1, waiting for transfers between devices, extended(): after = lax.ppermute(leading, axis, down)  31 us
    ppermute x1, waiting for transfers between devices, extended(): before = lax.ppermute(last, axis, up)  23.6 us
    unnamed x24, local copies, waits for them, and re-layouts  6.03 us
    dot_general x2, matrix products, complex_product(): jnp.einsum('spik,sqkj->spqij', left, right, preferred_element_type=jnp.fl...  5.85 us
    ppermute x7, starting transfers between devices, on_device(): ppermute(d_next, 'energy', [(to_i, (to_i + dev_i) % formed) for to_i in r...  5.15 us
    dot_general x1, matrix products, on_device(): jnp.dot(side_kernel, flat[0], preferred_element_type=jnp.float32)  5.02 us
  transfers between devices with their start and end apart: 9, of which 6 were waited for; matrix products, arithmetic and copies ran while one was open for 12% of the time, Pallas kernels for 0%

profile of v1, /device:TPU:0, one launch (start us, length us, event | category | flops | bytes accessed | tf_op | source)
XLA Modules:
  0.0 193.2 jit_solution(10999405325502706671)
XLA Ops:
  0.0 1.5 copy-done
  1.5 3.6 %convolution_bitcast_fusion.2 = f32[3,2,2,384,384]{3,4,1,2,0:T(8,128)S(1)} fusion(bf16[1,3,2,384,384]{4,3,2,1,0:T(8,128)(2,1)} %param.6, bf16[1,3,2,384,384]{4,3,2,1,0:T(8,128)(2,1)S(1)} %copy-done), kind=kOutput, calls=%fused_computation.7 | convolution fusion | flops 1358954496 | bytes 10616832 | tf_op jit(solution)/shard_map/spik,sqkj->spqij/dot_general | solution.py:22
  5.5 2.2 %convolution_bitcast_fusion.1 = f32[3,2,2,384,384]{4,3,2,1,0:T(8,128)S(1)} fusion(bf16[1,3,2,384,384]{4,3,2,1,0:T(8,128)(2,1)S(1)} %copy-done, bf16[3,1,384,384]{2,3,0,1:T(8,128)(2,1)S(1)} %fusion.19, bf16[3,1,384,384]{2,3,0,1:T(8,128)(2,1)S(1)} %fusion.18), kind=kOutput, calls=%fused_computation.6 | convolution fusion | flops 1359839232 | bytes 10616832 | tf_op jit(solution)/shard_map/spik,sqjk->spqij/dot_general | solution.py:27
  8.3 1.8 copy.72
  10.1 48.2 %all_to_all.18 = bf16[1,3,2,384,384]{4,2,1,0,3:T(2,128)(2,1)S(1)} all-to-all(bf16[1,3,2,384,384]{4,2,1,0,3:T(2,128)(2,1)S(1)} %copy.72), channel_id=1, replica_groups=mesh['atoms'=4,'energy'=8] {'energy'}, dimensions={3} | all-to-all | bytes 3538944 | tf_op jit(solution)/shard_map/all_to_all | solution.py:57
  58.8 4.6 %collective-permute-start = (bf16[1,24,2,48,384]{4,3,2,1,0:T(8,128)(2,1)S(1)}, bf16[1,24,2,48,384]{4,3,2,1,0:T(8,128)(2,1)}, u32[]{:S(2)}, u32[]{:S(2)}) collective-permute-start(bf16[1,24,2,48,384]{4,3,2,1,0:T(8,128)(2,1)S(1)} %bitcast.115), channel_id=1, source_target_pairs={{0,8},{8,16},{16,24},{1,9},{9,17},{17,25},{2,10},{10,18},{18,26},{... | collective-permute-start | bytes 5308424 | tf_op jit(solution)/shard_map/ppermute | solution.py:15
  64.2 0.7 reshape.325
  65.5 1.5 collective-permute-start.1
  67.0 0.7 fusion.35
  67.7 1.6 fusion.27
  69.9 2.2 %squeeze.14 = bf16[24,36864]{1,0:T(8,128)(2,1)} reshape(bf16[1,8,3,2,48,384]{5,4,3,2,1,0:T(8,128)(2,1)S(1)} %copy.74) | data formatting | bytes 3538944 | tf_op jit(solution)/shard_map/squeeze | solution.py:62
  72.1 4.0 %fusion.30 = f32[24,36864]{1,0:T(8,128)} fusion(bf16[24,36864]{1,0:T(8,128)(2,1)} %squeeze.14, f32[24,24]{1,0:T(8,128)} %get-tuple-element.6, f32[24]{0:T(128)S(1)} %compare_convert_fusion), kind=kOutput, calls=%fused_computation.71 | convolution fusion | flops 42469056 | bytes 5310816 | tf_op jit(solution)/shard_map/dot_general | solution.py:62
  76.1 23.6 %collective-permute-done = bf16[1,24,2,48,384]{4,3,2,1,0:T(8,128)(2,1)} collective-permute-done((bf16[1,24,2,48,384]{4,3,2,1,0:T(8,128)(2,1)S(1)}, bf16[1,24,2,48,384]{4,3,2,1,0:T(8,128)(2,1)}, u32[]{:S(2)}, u32[]{:S(2)}) %collective-permute-start) | collective-permute-done | bytes 1769504 | tf_op jit(solution)/shard_map/ppermute | solution.py:15
  99.7 3.9 %squeeze.15 = bf16[24,36864]{1,0:T(8,128)(2,1)} reshape(bf16[1,24,2,48,384]{4,3,2,1,0:T(8,128)(2,1)} %collective-permute-done) | data formatting | bytes 3538944 | tf_op jit(solution)/shard_map/squeeze | solution.py:63
  103.7 5.0 %convolution_add_fusion.1 = f32[24,36864]{1,0:T(8,128)} fusion(f32[24,36864]{1,0:T(8,128)} %fusion.30, bf16[24,36864]{1,0:T(8,128)(2,1)} %squeeze.15, f32[24,24]{1,0:T(8,128)S(1)} %get-tuple-element.5, f32[24]{0:T(128)S(1)} %compare_convert_fusion), kind=kOutput, calls=%fused_computation.1 | convolution fusion | flops 43353792 | bytes 8849760 | tf_op jit(solution)/shard_map/dot_general | solution.py:63
  108.7 31.0 %collective-permute-done.1 = bf16[1,24,2,48,384]{4,3,2,1,0:T(8,128)(2,1)} collective-permute-done((bf16[1,24,2,48,384]{4,3,2,1,0:T(8,128)(2,1)S(1)}, bf16[1,24,2,48,384]{4,3,2,1,0:T(8,128)(2,1)}, u32[]{:S(2)}, u32[]{:S(2)}) %collective-permute-start.1) | collective-permute-done | bytes 1769504 | tf_op jit(solution)/shard_map/ppermute | solution.py:16
  139.7 2.7 %squeeze.16 = bf16[24,36864]{1,0:T(8,128)(2,1)S(1)} reshape(bf16[1,24,2,48,384]{4,3,2,1,0:T(8,128)(2,1)} %collective-permute-done.1) | data formatting | bytes 3538944 | tf_op jit(solution)/shard_map/squeeze | solution.py:64
  142.4 2.7 %fusion = bf16[24,36864]{1,0:T(8,128)(2,1)S(1)} fusion(f32[24,36864]{1,0:T(8,128)} %convolution_add_fusion.1, bf16[24,36864]{1,0:T(8,128)(2,1)S(1)} %squeeze.16, f32[24,24]{1,0:T(8,128)S(1)} %get-tuple-element.5, f32[24]{0:T(128)S(1)} %compare_convert_fusion), kind=kOutput, calls=%fused_computation.2 | convolution fusion | flops 44238528 | bytes 7080288 | tf_op jit(solution)/shard_map/dot_general | solution.py:64
  145.3 0.8 fusion.1
  146.1 1.2 fusion.38
  147.9 1.2 collective-permute-start.3
  149.9 3.4 %collective-permute-done.2 = bf16[1,3,2,48,384]{4,3,2,1,0:T(8,128)(2,1)} collective-permute-done((bf16[1,3,2,48,384]{4,3,2,1,0:T(8,128)(2,1)}, bf16[1,3,2,48,384]{4,3,2,1,0:T(8,128)(2,1)}, u32[]{:S(2)}, u32[]{:S(2)}) %collective-permute-start.2) | collective-permute-done | bytes 221216 | tf_op jit(solution)/shard_map/ppermute | solution.py:73
  153.3 2.5 %collective-permute-start.4 = (bf16[1,3,2,48,384]{4,3,2,1,0:T(8,128)(2,1)}, bf16[1,3,2,48,384]{4,3,2,1,0:T(8,128)(2,1)S(1)}, u32[]{:S(2)}, u32[]{:S(2)}) collective-permute-start(bf16[1,3,2,48,384]{4,3,2,1,0:T(8,128)(2,1)} %get-tuple-element.11), channel_id=1, source_target_pairs={{0,5},{1,6},{2,7},{3,0},{4,1},{5,2},{6,3},{7,4},{8,13},{9,14},{10,... | collective-permute-start | bytes 663560 | tf_op jit(solution)/shard_map/ppermute | solution.py:73
  155.8 1.0 constant_dynamic-update-slice_fusion.13
  156.8 11.3 %collective-permute-done.3 = bf16[1,3,2,48,384]{4,3,2,1,0:T(8,128)(2,1)} collective-permute-done((bf16[1,3,2,48,384]{4,3,2,1,0:T(8,128)(2,1)}, bf16[1,3,2,48,384]{4,3,2,1,0:T(8,128)(2,1)}, u32[]{:S(2)}, u32[]{:S(2)}) %collective-permute-start.3) | collective-permute-done | bytes 221216 | tf_op jit(solution)/shard_map/ppermute | solution.py:73
  168.1 1.0 constant_dynamic-update-slice_fusion.12
  169.1 3.2 %collective-permute-done.4 = bf16[1,3,2,48,384]{4,3,2,1,0:T(8,128)(2,1)S(1)} collective-permute-done((bf16[1,3,2,48,384]{4,3,2,1,0:T(8,128)(2,1)}, bf16[1,3,2,48,384]{4,3,2,1,0:T(8,128)(2,1)S(1)}, u32[]{:S(2)}, u32[]{:S(2)}) %collective-permute-start.4) | collective-permute-done | bytes 221216 | tf_op jit(solution)/shard_map/ppermute | solution.py:73
  172.4 13.2 %collective-permute-done.5 = bf16[1,3,2,48,384]{4,3,2,1,0:T(8,128)(2,1)S(1)} collective-permute-done((bf16[1,3,2,48,384]{4,3,2,1,0:T(8,128)(2,1)}, bf16[1,3,2,48,384]{4,3,2,1,0:T(8,128)(2,1)S(1)}, u32[]{:S(2)}, u32[]{:S(2)}) %collective-permute-start.5) | collective-permute-done | bytes 221216 | tf_op jit(solution)/shard_map/ppermute | solution.py:73
  185.8 1.0 constant_dynamic-update-slice_fusion.6
  186.8 1.0 constant_dynamic-update-slice_fusion.5
  188.1 2.2 %convolution_bitcast_fusion = f32[3,2,2,384,384]{3,4,1,2,0:T(8,128)S(1)} fusion(bf16[1,3,2,384,384]{4,3,2,1,0:T(8,128)(2,1)S(1)} %copy-done, bf16[1,3,2,768,384]{4,3,2,1,0:T(8,128)(2,1)S(1)} %slice_dynamic-update-slice_fusion.1, s32[]{:T(128)S(6)} %select_n.49), kind=kOutput, calls=%fused_computation.5 | convolution fusion | flops 1358954496 | bytes 10616836 | tf_op jit(solution)/shard_map/spik,sqkj->spqij/dot_general | solution.py:22
  190.9 2.3 %copy.79 = bf16[1,3,2,384,384]{4,3,2,1,0:T(8,128)(2,1)} copy(bf16[1,3,2,384,384]{3,4,1,2,0:T(8,128)(2,1)S(1)} %pad_maximum_fusion.1) | data formatting | bytes 3538944 | tf_op jit(solution)/shard_map/stack | solution.py:23
  (47 shorter events, 6.3 us)
Async XLA Ops:
  0.0 1.5 copy-start
  58.5 4.8 %copy-start.3 = (s32[8]{0:T(128)S(1)}, s32[8]{0:T(128)}, u32[]{:S(2)}) copy-start(s32[8]{0:T(128)} %param.7) | copy-start | bytes 100
  58.6 5.0 %copy-start.2 = (s32[64]{0:T(128)S(1)}, s32[64]{0:T(128)}, u32[]{:S(2)}) copy-start(s32[64]{0:T(128)} %param.8) | copy-start | bytes 772
  58.6 9.1 %copy-start.1 = (f32[4,64]{1,0:T(4,128)S(1)}, f32[4,64]{1,0:T(4,128)}, u32[]{:S(2)}) copy-start(f32[4,64]{1,0:T(4,128)} %param.9) | copy-start | bytes 3076
  58.8 41.0 %collective-permute-start = (bf16[1,24,2,48,384]{4,3,2,1,0:T(8,128)(2,1)S(1)}, bf16[1,24,2,48,384]{4,3,2,1,0:T(8,128)(2,1)}, u32[]{:S(2)}, u32[]{:S(2)}) collective-permute-start(bf16[1,24,2,48,384]{4,3,2,1,0:T(8,128)(2,1)S(1)} %bitcast.115), channel_id=1, source_target_pairs={{0,8},{8,16},{16,24},{1,9},{9,17},{17,25},{2,10},{10,18},{18,26},{... | collective-permute-start | bytes 5308424 | tf_op jit(solution)/shard_map/ppermute | solution.py:15
  65.5 74.2 %collective-permute-start.1 = (bf16[1,24,2,48,384]{4,3,2,1,0:T(8,128)(2,1)S(1)}, bf16[1,24,2,48,384]{4,3,2,1,0:T(8,128)(2,1)}, u32[]{:S(2)}, u32[]{:S(2)}) collective-permute-start(bf16[1,24,2,48,384]{4,3,2,1,0:T(8,128)(2,1)S(1)} %bitcast.116), channel_id=1, source_target_pairs={{8,0},{16,8},{24,16},{9,1},{17,9},{25,17},{10,2},{18,10},{26,18},{... | collective-permute-start | bytes 5308424 | tf_op jit(solution)/shard_map/ppermute | solution.py:16
  147.3 6.1 %collective-permute-start.2 = (bf16[1,3,2,48,384]{4,3,2,1,0:T(8,128)(2,1)}, bf16[1,3,2,48,384]{4,3,2,1,0:T(8,128)(2,1)}, u32[]{:S(2)}, u32[]{:S(2)}) collective-permute-start(bf16[1,3,2,48,384]{4,3,2,1,0:T(8,128)(2,1)} %get-tuple-element.13), channel_id=1, source_target_pairs={{0,7},{1,0},{2,1},{3,2},{4,3},{5,4},{6,5},{7,6},{8,15},{9,8},{10,9... | collective-permute-start | bytes 663560 | tf_op jit(solution)/shard_map/ppermute | solution.py:73
  147.9 20.3 %collective-permute-start.3 = (bf16[1,3,2,48,384]{4,3,2,1,0:T(8,128)(2,1)}, bf16[1,3,2,48,384]{4,3,2,1,0:T(8,128)(2,1)}, u32[]{:S(2)}, u32[]{:S(2)}) collective-permute-start(bf16[1,3,2,48,384]{4,3,2,1,0:T(8,128)(2,1)} %get-tuple-element.12), channel_id=1, source_target_pairs={{0,6},{1,7},{2,0},{3,1},{4,2},{5,3},{6,4},{7,5},{8,14},{9,15},{10,... | collective-permute-start | bytes 663560 | tf_op jit(solution)/shard_map/ppermute | solution.py:73
  149.1 36.7 %collective-permute-start.8 = (bf16[1,3,2,48,384]{4,3,2,1,0:T(8,128)(2,1)}, bf16[1,3,2,48,384]{4,3,2,1,0:T(8,128)(2,1)S(1)}, u32[]{:S(2)}, u32[]{:S(2)}) collective-permute-start(bf16[1,3,2,48,384]{4,3,2,1,0:T(8,128)(2,1)} %get-tuple-element.7), channel_id=1, source_target_pairs={{0,1},{1,2},{2,3},{3,4},{4,5},{5,6},{6,7},{7,0},{8,9},{9,10},{10,1... | collective-permute-start | bytes 663560 | tf_op jit(solution)/shard_map/ppermute | solution.py:73
  149.3 36.4 %collective-permute-start.7 = (bf16[1,3,2,48,384]{4,3,2,1,0:T(8,128)(2,1)}, bf16[1,3,2,48,384]{4,3,2,1,0:T(8,128)(2,1)S(1)}, u32[]{:S(2)}, u32[]{:S(2)}) collective-permute-start(bf16[1,3,2,48,384]{4,3,2,1,0:T(8,128)(2,1)} %get-tuple-element.8), channel_id=1, source_target_pairs={{0,2},{1,3},{2,4},{3,5},{4,6},{5,7},{6,0},{7,1},{8,10},{9,11},{10,... | collective-permute-start | bytes 663560 | tf_op jit(solution)/shard_map/ppermute | solution.py:73
  149.9 35.7 %collective-permute-start.6 = (bf16[1,3,2,48,384]{4,3,2,1,0:T(8,128)(2,1)}, bf16[1,3,2,48,384]{4,3,2,1,0:T(8,128)(2,1)S(1)}, u32[]{:S(2)}, u32[]{:S(2)}) collective-permute-start(bf16[1,3,2,48,384]{4,3,2,1,0:T(8,128)(2,1)} %get-tuple-element.9), channel_id=1, source_target_pairs={{0,3},{1,4},{2,5},{3,6},{4,7},{5,0},{6,1},{7,2},{8,11},{9,12},{10,... | collective-permute-start | bytes 663560 | tf_op jit(solution)/shard_map/ppermute | solution.py:73
  153.3 19.0 %collective-permute-start.4 = (bf16[1,3,2,48,384]{4,3,2,1,0:T(8,128)(2,1)}, bf16[1,3,2,48,384]{4,3,2,1,0:T(8,128)(2,1)S(1)}, u32[]{:S(2)}, u32[]{:S(2)}) collective-permute-start(bf16[1,3,2,48,384]{4,3,2,1,0:T(8,128)(2,1)} %get-tuple-element.11), channel_id=1, source_target_pairs={{0,5},{1,6},{2,7},{3,0},{4,1},{5,2},{6,3},{7,4},{8,13},{9,14},{10,... | collective-permute-start | bytes 663560 | tf_op jit(solution)/shard_map/ppermute | solution.py:73
  168.1 17.5 %collective-permute-start.5 = (bf16[1,3,2,48,384]{4,3,2,1,0:T(8,128)(2,1)}, bf16[1,3,2,48,384]{4,3,2,1,0:T(8,128)(2,1)S(1)}, u32[]{:S(2)}, u32[]{:S(2)}) collective-permute-start(bf16[1,3,2,48,384]{4,3,2,1,0:T(8,128)(2,1)} %get-tuple-element.10), channel_id=1, source_target_pairs={{0,4},{1,5},{2,6},{3,7},{4,0},{5,1},{6,2},{7,3},{8,12},{9,13},{10,... | collective-permute-start | bytes 663560 | tf_op jit(solution)/shard_map/ppermute | solution.py:73
